TPU v7x, 32 devices: a whole 2x2x4 slice. The times are simulated.
32 devices in a mesh: dp: 4 (over y, core), ep: 8 (over z, x).
Axes of the slice: x: 2, y: 2, z: 4, core: 2. Of those that a mesh axis runs over, the one named last changes fastest.
Arguments:
- tokens: bfloat16 [32, 256, 2048], P(('dp', 'ep')), may hold values from -6 to 6
- lengths: int32 [32], P(('dp', 'ep')), may hold values from 64 to 256, as said below
- routes: int32 [32, 256, 8], P(('dp', 'ep')), may hold values from 0 to 15, all different within a row
- pair_order: int32 [32, 2048], P(('dp', 'ep')), may hold values from 0 to 2047, each once within a row
- gate_weights: float32 [32, 256, 8], P(('dp', 'ep')), may hold values from 0.05 to 0.5
- attn_weight: bfloat16 [2048, 8192], P(('dp', 'ep')), may hold values from -0.375 to 0.375
- gains: float32 [4352], replicated, may hold values from 0.5 to 1.5
- expert_gate_up: bfloat16 [16, 2048, 2048], P('ep'), may hold values from -0.125 to 0.125
- expert_down: bfloat16 [16, 1024, 2048], P('ep'), may hold values from -0.375 to 0.375
- cotangent: bfloat16 [32, 256, 2048], P(('dp', 'ep')), may hold values from -6 to 6
Outputs:
- output: bfloat16 [32, 256, 2048], P(('dp', 'ep'))
- input_grad: float32 [32, 256, 2048], P(('dp', 'ep'))
- attn_weight_grad: float32 [2048, 8192], P(('dp', 'ep'))
- gains_grad: float32 [4352], P(('dp', 'ep'))
- gate_up_grad: float32 [16, 2048, 2048], P('ep', 'dp')
- down_grad: float32 [16, 1024, 2048], P('ep', 'dp')
Inputs may be any that keep to these rules, and one draw needn't show every extreme that they name: `lengths`: slots at or beyond a sequence's length are padding; in every draw some sequence fills all 256 slots. `routes`: the 8 experts of a slot are distinct. `pair_order`: within each sequence every value appears once.
All inputs are finite; a program needn't handle non-finite values.
Results may differ from a plain program's by a relative error of at most 0.014.
Values may be sent and summed in bfloat16 or wider, within the bound.
No kernel may reach another device: no remote copies, remote signals or barrier semaphores. Data moves between devices by JAX's collectives and lax.ppermute only.
A program may use at most 448 MiB of HBM per device.

v0:
```python
import math
import jax
import jax.numpy as jnp
from jax import lax
from jax.sharding import PartitionSpec as P

HEAD = 128
EPS = 1e-06
THETA = 10000.0
NEG = -1e30


def inv_rms(values):
    return lax.rsqrt(jnp.mean(values * values, axis=-1, keepdims=True) + EPS)


def norm_back(values, inv_scale, gain_vec, grad_in):
    scaled = grad_in * gain_vec
    mean_term = jnp.mean(scaled * values, axis=-1, keepdims=True)
    return inv_scale * scaled - values * (inv_scale * inv_scale * inv_scale) * mean_term


def rope_tables(slot_count, head_size):
    half_size = head_size // 2
    frequency = THETA ** (-(jnp.arange(half_size, dtype=jnp.float32) * 2.0) / head_size)
    angles = jnp.arange(slot_count, dtype=jnp.float32)[:, None] * frequency[None, :]
    return (jnp.cos(angles)[:, None, :], jnp.sin(angles)[:, None, :])


def rotary(values, cosine_table, sine_table):
    half_size = values.shape[-1] // 2
    first_half = values[..., :half_size]
    second_half = values[..., half_size:]
    return jnp.concatenate(
        [
            first_half * cosine_table - second_half * sine_table,
            second_half * cosine_table + first_half * sine_table,
        ],
        axis=-1,
    )


def rotary_back(grad_in, cosine_table, sine_table):
    half_size = grad_in.shape[-1] // 2
    first_half = grad_in[..., :half_size]
    second_half = grad_in[..., half_size:]
    return jnp.concatenate(
        [
            first_half * cosine_table + second_half * sine_table,
            second_half * cosine_table - first_half * sine_table,
        ],
        axis=-1,
    )


def on_device(
    tokens,
    lengths,
    routes,
    pair_order,
    gate_weights,
    attn_weight,
    gains,
    expert_gate_up,
    expert_down,
    cotangent,
):
    slot_count = tokens.shape[1]
    model_width = tokens.shape[2]
    head_size = HEAD
    head_count = model_width // head_size
    top_count = routes.shape[2]
    experts_dev = expert_gate_up.shape[0]
    hidden_units = expert_down.shape[1]
    groups = lax.axis_size("ep")
    experts = experts_dev * groups
    capacity = (9 * slot_count * top_count + 8 * experts - 1) // (8 * experts)
    pair_count = slot_count * top_count
    factor = 1.0 / math.sqrt(head_size)
    inputs = tokens[0].astype(jnp.float32)
    length = lengths[0]
    slot_live = jnp.arange(slot_count) < length
    live_rows = slot_live.astype(jnp.float32)[:, None]
    gain_attn = gains[:model_width]
    gain_ffn = gains[model_width : 2 * model_width]
    gain_query = gains[2 * model_width : 2 * model_width + head_size]
    gain_key = gains[2 * model_width + head_size :]
    whole_weight = lax.all_gather(attn_weight, ("dp", "ep"), axis=0, tiled=True)
    weight_qkv = whole_weight[:, : 3 * model_width]
    weight_out = whole_weight[:, 3 * model_width :]
    scale_first = inv_rms(inputs)
    xn_first = (inputs * scale_first * gain_attn).astype(jnp.bfloat16)
    projected = jnp.dot(xn_first, weight_qkv, preferred_element_type=jnp.float32)
    query_raw = projected[:, :model_width].reshape(slot_count, head_count, head_size)
    key_raw = projected[:, model_width : 2 * model_width].reshape(slot_count, head_count, head_size)
    values_low = (
        projected[:, 2 * model_width :]
        .astype(jnp.bfloat16)
        .reshape(slot_count, head_count, head_size)
    )
    cosine_table, sine_table = rope_tables(slot_count, head_size)
    query_scale = inv_rms(query_raw)
    key_scale = inv_rms(key_raw)
    query_rot = rotary(query_raw * query_scale * gain_query, cosine_table, sine_table).astype(
        jnp.bfloat16
    )
    key_rot = rotary(key_raw * key_scale * gain_key, cosine_table, sine_table).astype(jnp.bfloat16)

    def score_table():
        raw_scores = (
            jnp.einsum("qhd,khd->hqk", query_rot, key_rot, preferred_element_type=jnp.float32)
            * factor
        )
        return jnp.where(slot_live[None, None, :], raw_scores, NEG)

    scores = score_table()
    row_max = jnp.max(scores, axis=-1, keepdims=True)
    log_total = row_max + jnp.log(jnp.sum(jnp.exp(scores - row_max), axis=-1, keepdims=True))
    probs_low = jnp.exp(scores - log_total).astype(jnp.bfloat16)
    attended = jnp.einsum("hqk,khd->qhd", probs_low, values_low, preferred_element_type=jnp.float32)
    attended = attended.reshape(slot_count, model_width).astype(jnp.bfloat16)
    resid = inputs + jnp.dot(attended, weight_out, preferred_element_type=jnp.float32)
    scale_second = inv_rms(resid)
    xn_second = (resid * scale_second * gain_ffn).astype(jnp.bfloat16)
    expert_flat = routes[0].reshape(pair_count)
    order_row = pair_order[0]
    pair_index = jnp.arange(pair_count, dtype=jnp.int32)
    pair_live = pair_index // top_count < length
    by_rank = jnp.zeros((pair_count,), jnp.int32).at[order_row].set(pair_index)
    one_hot = (
        (expert_flat[by_rank][:, None] == jnp.arange(experts, dtype=jnp.int32)[None, :])
        & pair_live[by_rank][:, None]
    ).astype(jnp.int32)
    earlier = jnp.cumsum(one_hot, axis=0) - one_hot
    pair_rank = jnp.sum(earlier * one_hot, axis=1)[order_row]
    kept_pair = pair_live & (pair_rank < capacity)
    dest_slot = jnp.where(kept_pair, expert_flat * capacity + pair_rank, experts * capacity)
    source = (
        jnp.full((experts * capacity + 1,), pair_count, jnp.int32).at[dest_slot].set(pair_index)
    )
    source = source[: experts * capacity]
    source_token = source // top_count
    xn_ext = jnp.concatenate([xn_second, jnp.zeros((1, model_width), jnp.bfloat16)], axis=0)
    send_rows = xn_ext[source_token].reshape(groups, experts_dev, capacity, model_width)
    received = lax.all_to_all(send_rows, "ep", split_axis=0, concat_axis=0, tiled=True)
    gate_up = jnp.einsum(
        "sjcd,jdf->sjcf", received, expert_gate_up, preferred_element_type=jnp.float32
    )
    activation = (jax.nn.silu(gate_up[..., :hidden_units]) * gate_up[..., hidden_units:]).astype(
        jnp.bfloat16
    )
    result = jnp.einsum(
        "sjcf,jfd->sjcd", activation, expert_down, preferred_element_type=jnp.float32
    )
    returned = lax.all_to_all(
        result.astype(jnp.bfloat16), "ep", split_axis=0, concat_axis=0, tiled=True
    )
    returned, received, gate_up, activation = (returned, received, gate_up, activation)
    back_ext = jnp.concatenate(
        [
            returned.reshape(experts * capacity, model_width),
            jnp.zeros((1, model_width), jnp.bfloat16),
        ],
        axis=0,
    )
    weight = jnp.where(kept_pair, gate_weights[0].reshape(pair_count), 0.0)
    mixed = jnp.sum(
        (back_ext[dest_slot].astype(jnp.float32) * weight[:, None]).reshape(
            slot_count, top_count, model_width
        ),
        axis=1,
    )
    output = (live_rows * (resid + mixed)).astype(jnp.bfloat16)
    grad_out = cotangent[0].astype(jnp.float32) * live_rows
    grad_ext = jnp.concatenate([grad_out, jnp.zeros((1, model_width), jnp.float32)], axis=0)
    weight_ext = jnp.concatenate([weight, jnp.zeros((1,), jnp.float32)], axis=0)
    slot_grad = (grad_ext[source_token] * weight_ext[source][:, None]).astype(jnp.bfloat16)
    slot_grad = slot_grad.reshape(groups, experts_dev, capacity, model_width)
    grad_recv = lax.all_to_all(slot_grad, "ep", split_axis=0, concat_axis=0, tiled=True)
    grad_act = jnp.einsum(
        "sjcd,jfd->sjcf", grad_recv, expert_down, preferred_element_type=jnp.float32
    )
    grad_down = jnp.einsum(
        "sjcf,sjcd->jfd", activation, grad_recv, preferred_element_type=jnp.float32
    )
    gate_part = gate_up[..., :hidden_units]
    up_part = gate_up[..., hidden_units:]
    sigmoid_gate = jax.nn.sigmoid(gate_part)
    grad_gate = grad_act * up_part * sigmoid_gate * (1.0 + gate_part * (1.0 - sigmoid_gate))
    grad_up = grad_act * gate_part * sigmoid_gate
    grad_gate_up = jnp.concatenate([grad_gate, grad_up], axis=-1).astype(jnp.bfloat16)
    grad_weight_gu = jnp.einsum(
        "sjcd,sjcf->jdf", received, grad_gate_up, preferred_element_type=jnp.float32
    )
    grad_rows = jnp.einsum(
        "sjcf,jdf->sjcd", grad_gate_up, expert_gate_up, preferred_element_type=jnp.float32
    )
    rows_back = lax.all_to_all(
        grad_rows.astype(jnp.bfloat16), "ep", split_axis=0, concat_axis=0, tiled=True
    )
    rows_ext = jnp.concatenate(
        [
            rows_back.reshape(experts * capacity, model_width),
            jnp.zeros((1, model_width), jnp.bfloat16),
        ],
        axis=0,
    )
    grad_xn_second = jnp.sum(
        rows_ext[dest_slot].astype(jnp.float32).reshape(slot_count, top_count, model_width), axis=1
    )
    expert_sums = (
        lax.psum_scatter(grad_weight_gu, "dp", scatter_dimension=1, tiled=True),
        lax.psum_scatter(grad_down, "dp", scatter_dimension=1, tiled=True),
    )
    grad_resid = grad_out + norm_back(resid, scale_second, gain_ffn, grad_xn_second)
    grad_gain_ffn = jnp.sum(grad_xn_second * resid * scale_second, axis=0)
    grad_branch = grad_resid.astype(jnp.bfloat16)
    grad_wout = jnp.einsum("sa,sb->ab", attended, grad_branch, preferred_element_type=jnp.float32)
    grad_att = jnp.einsum("sb,ab->sa", grad_branch, weight_out, preferred_element_type=jnp.float32)
    grad_att = grad_att.astype(jnp.bfloat16).reshape(slot_count, head_count, head_size)
    scores_again = score_table()
    probs_again = jnp.exp(scores_again - log_total)
    grad_probs = jnp.einsum(
        "qhd,khd->hqk", grad_att, values_low, preferred_element_type=jnp.float32
    )
    grad_values = jnp.einsum(
        "hqk,qhd->khd",
        probs_again.astype(jnp.bfloat16),
        grad_att,
        preferred_element_type=jnp.float32,
    )
    grad_values = grad_values.astype(jnp.bfloat16)
    inner_sum = jnp.sum(probs_again * grad_probs, axis=-1, keepdims=True)
    grad_scores = (probs_again * (grad_probs - inner_sum)).astype(jnp.bfloat16)
    grad_qrot = (
        jnp.einsum("hqk,khd->qhd", grad_scores, key_rot, preferred_element_type=jnp.float32)
        * factor
    )
    grad_krot = (
        jnp.einsum("hqk,qhd->khd", grad_scores, query_rot, preferred_element_type=jnp.float32)
        * factor
    )
    grad_qnorm = rotary_back(grad_qrot, cosine_table, sine_table)
    grad_knorm = rotary_back(grad_krot, cosine_table, sine_table)
    grad_query = norm_back(query_raw, query_scale, gain_query, grad_qnorm).astype(jnp.bfloat16)
    grad_key = norm_back(key_raw, key_scale, gain_key, grad_knorm).astype(jnp.bfloat16)
    grad_gain_query = jnp.sum(grad_qnorm * query_raw * query_scale, axis=(0, 1))
    grad_gain_key = jnp.sum(grad_knorm * key_raw * key_scale, axis=(0, 1))
    grad_proj = jnp.concatenate(
        [
            grad_query.reshape(slot_count, model_width),
            grad_key.reshape(slot_count, model_width),
            grad_values.reshape(slot_count, model_width),
        ],
        axis=1,
    )
    grad_wqkv = jnp.einsum("sa,sb->ab", xn_first, grad_proj, preferred_element_type=jnp.float32)
    grad_xn_first = jnp.einsum(
        "sb,ab->sa", grad_proj, weight_qkv, preferred_element_type=jnp.float32
    )
    input_grad = grad_resid + norm_back(inputs, scale_first, gain_attn, grad_xn_first)
    grad_gain_attn = jnp.sum(grad_xn_first * inputs * scale_first, axis=0)
    gain_terms = jnp.concatenate(
        [grad_gain_attn, grad_gain_ffn, grad_gain_query, grad_gain_key], axis=0
    )
    full_terms = jnp.concatenate([grad_wqkv, grad_wout], axis=1)
    attn_share, gain_share = (
        lax.psum_scatter(full_terms, ("dp", "ep"), scatter_dimension=0, tiled=True),
        lax.psum_scatter(gain_terms, ("dp", "ep"), scatter_dimension=0, tiled=True),
    )
    return (output[None], input_grad[None], attn_share, gain_share, expert_sums[0], expert_sums[1])


def solution(mesh):
    in_specs = (
        P(("dp", "ep"), None, None),
        P(("dp", "ep")),
        P(("dp", "ep"), None, None),
        P(("dp", "ep"), None),
        P(("dp", "ep"), None, None),
        P(("dp", "ep"), None),
        P(),
        P("ep", None, None),
        P("ep", None, None),
        P(("dp", "ep"), None, None),
    )
    out_specs = (
        P(("dp", "ep"), None, None),
        P(("dp", "ep"), None, None),
        P(("dp", "ep"), None),
        P(("dp", "ep")),
        P("ep", "dp", None),
        P("ep", "dp", None),
    )
    return jax.shard_map(
        on_device, mesh=mesh, in_specs=in_specs, out_specs=out_specs, check_vma=False
    )
```

profile of v0, /device:TPU:0, one launch (start us, length us, event | category | flops | bytes accessed | tf_op | source)
XLA Modules:
  0.0 2815.4 jit_solution(5414634431829395121)
XLA Ops:
  11.2 8.0 scatter_custom_fusion
  19.2 13.1 gather_fusion.1
  32.3 11.8 gather_fusion
  44.2 4.6 reduce-window.6
  49.5 11.8 gather_fusion.2
  61.4 8.1 scatter_custom_fusion.1
  73.3 135.3 %all-gather.2.cloned.1.call-done = bf16[2048,8192]{1,0:T(8,128)(2,1)} async-done(((bf16[64,8192]{1,0:T(8,128)(2,1)}), bf16[2048,8192]{1,0:T(8,128)(2,1)}) %all-gather.2.cloned.1.call-update) | async-done | bytes 33554448 | tf_op jit(solution)/shard_map/all_gather | solution.py:88
  208.5 11.7 fusion.2
  220.3 3.4 slice_bitcast_fusion.3
  242.6 6.2 multiply_reduce_fusion.3
  250.2 9.8 gather_fusion.3
  260.0 5.2 all-to-all-start
  266.1 12.3 gather_fusion.6
  279.1 11.5 gather_fusion.5
  290.6 9.9 multiply_convert_fusion
  300.5 171.0 %all-to-all-done = bf16[8,2,144,2048]{3,2,1,0:T(8,128)(2,1)} async-done(((bf16[8,2,144,2048]{3,2,1,0:T(8,128)(2,1)}), bf16[8,2,144,2048]{3,2,1,0:T(8,128)(2,1)}, u32[]{:S(2)}, u32[]{:S(2)}) %all-to-all-start) | async-done | bytes 9437216 | tf_op jit(solution)/shard_map/all_to_all | solution.py:145
  471.5 5.1 all-to-all-start.2
  476.6 27.8 fusion.27
  504.4 177.6 %all-to-all-done.2 = bf16[8,2,144,2048]{3,2,1,0:T(8,128)(2,1)} async-done(((bf16[8,2,144,2048]{3,2,1,0:T(8,128)(2,1)}), bf16[8,2,144,2048]{3,2,1,0:T(8,128)(2,1)}, u32[]{:S(2)}, u32[]{:S(2)}) %all-to-all-start.2) | async-done | bytes 9437216 | tf_op jit(solution)/shard_map/all_to_all | solution.py:179
  682.0 22.7 fusion.11
  704.7 18.3 fusion.32
  723.0 30.6 %convolution_bitcast_fusion = f32[2,2048,2048]{2,1,0:T(8,128)} fusion(bf16[8,2,144,2048]{3,2,1,0:T(8,128)(2,1)} %all-to-all-done, bf16[8,2,144,1024]{3,2,0,1:T(8,128)(2,1)} %get-tuple-element.15, bf16[8,2,144,1024]{3,2,0,1:T(8,128)(2,1)} %get-tuple-element.14), kind=kOutput, calls=%fused_computation.23 | convolution fusion | flops 19346227200 | bytes 52428800 | tf_op jit(solution)/shard_map/sjcd,sjcf->jdf/dot_general | solution.py:192
  753.7 17.2 convert_bitcast_fusion.1
  770.8 9.3 copy.197
  780.1 5.3 all-to-all-start.1
  785.4 25.9 convert_bitcast_fusion
  811.3 9.3 copy.202
  820.6 169.2 %all-to-all-done.1 = bf16[8,2,144,2048]{3,2,1,0:T(8,128)(2,1)} async-done(((bf16[8,2,144,2048]{3,2,1,0:T(8,128)(2,1)}), bf16[8,2,144,2048]{3,2,1,0:T(8,128)(2,1)}, u32[]{:S(2)}, u32[]{:S(2)}) %all-to-all-start.1) | async-done | bytes 9437216 | tf_op jit(solution)/shard_map/all_to_all | solution.py:155
  989.9 5.1 all-to-all-start.3
  997.8 9.3 concatenate.49
  1007.0 192.4 %all-to-all-done.3 = bf16[8,2,144,2048]{3,2,1,0:T(8,128)(2,1)} async-done(((bf16[8,2,144,2048]{3,2,1,0:T(8,128)(2,1)}), bf16[8,2,144,2048]{3,2,1,0:T(8,128)(2,1)}, u32[]{:S(2)}, u32[]{:S(2)}) %all-to-all-start.3) | async-done | bytes 9437216 | tf_op jit(solution)/shard_map/all_to_all | solution.py:198
  1199.4 9.2 concatenate.53
  1208.7 21.3 gather_fusion.4
  1229.9 21.6 gather_fusion.7
  1251.6 11.4 convert_reduce_fusion
  1266.3 12.7 fusion.4
  1279.1 4.1 subtract_add_fusion
  1284.5 5.7 fusion.42
  1296.0 4.3 multiply_reduce_fusion
  1310.5 4.9 fusion.74
  1316.1 9.9 fusion.76
  1331.3 9.0 fusion.61
  1340.3 21.3 fusion.66
  1361.6 43.4 %pad_maximum_fusion = f32[2048,8192]{1,0:T(8,128)} fusion(f32[2048,2048]{1,0:T(8,128)} %fusion.76, f32[2048,6144]{1,0:T(8,128)} %fusion.66), kind=kLoop, calls=%fused_computation.10 | loop fusion | flops 16777216 | bytes 134217728 | tf_op jit(solution)/shard_map/concatenate | solution.py:266
  1405.1 14.7 fusion.55
  1419.9 47.2 %all-reduce.4 = f32[4352]{0:T(1024)S(1)} all-reduce(f32[4352]{0:T(1024)S(1)} %pad_maximum_fusion.13), channel_id=3, replica_groups=mesh['dp'=4,'ep'=8] {'dp','ep'}, use_global_device_ids=true, to_apply=%region_25.26.clone | all-reduce | flops 4352 | bytes 34816
  1467.7 3.5 fusion.52
  1471.2 1337.2 %reduce-scatter.4.cloned.1.call-done = f32[64,8192]{1,0:T(8,128)} async-done(((f32[2048,8192]{1,0:T(8,128)}), f32[64,8192]{1,0:T(8,128)}) %reduce-scatter.4.cloned.1.call-update) | async-done | bytes 2097168 | tf_op jit(solution)/shard_map/reduce_scatter | solution.py:268
  (240 shorter events, 59.4 us)
Async XLA Ops:
  7.2 201.4 %all-gather.2.cloned.1.call-start = ((), (), s32[]{:S(2)}) async-start(), calls=%async_computation.7 | async-start | bytes 34603008 | tf_op jit(solution)/shard_map/all_gather | solution.py:88
  49.5 21.2 copy-start.9
  49.5 22.0 copy-start.61
  61.3 147.2 %copy-start.43 = (s32[2048]{0:T(1024)}, s32[2048]{0:T(1024)S(1)}, u32[]{:S(2)}) copy-start(s32[2048]{0:T(1024)S(1)} %gather_fusion.2) | copy-start | bytes 24580
  61.4 10.2 copy-start.55
  71.6 137.0 %copy-start.45 = (f32[256]{0:T(256)}, f32[256]{0:T(256)S(1)}, u32[]{:S(2)}) copy-start(f32[256]{0:T(256)S(1)} %get-tuple-element.52) | copy-start | bytes 3076
  72.8 135.8 %copy-start.29 = (f32[2048]{0:T(1024)}, f32[2048]{0:T(1024)S(1)}, u32[]{:S(2)}) copy-start(f32[2048]{0:T(1024)S(1)} %get-tuple-element.42) | copy-start | bytes 24580
  73.3 161.2 %copy-start.25 = (f32[256,64]{1,0:T(8,128)}, f32[256,64]{1,0:T(8,128)S(1)}, u32[]{:S(2)}) copy-start(f32[256,64]{1,0:T(8,128)S(1)} %get-tuple-element.55) | copy-start | bytes 196612
  73.3 161.2 %copy-start.27 = (f32[256,64]{1,0:T(8,128)}, f32[256,64]{1,0:T(8,128)S(1)}, u32[]{:S(2)}) copy-start(f32[256,64]{1,0:T(8,128)S(1)} %get-tuple-element.56) | copy-start | bytes 196612
  224.1 7.6 copy-start.5
  227.1 4.6 copy-start.36
  242.6 6.2 copy-start.21
  242.6 6.9 copy-start.40
  260.0 5.2 copy-start.53
  260.0 5.5 copy-start.44
  260.0 6.1 copy-start.49
  260.0 211.5 %all-to-all-start = ((bf16[8,2,144,2048]{3,2,1,0:T(8,128)(2,1)}), bf16[8,2,144,2048]{3,2,1,0:T(8,128)(2,1)}, u32[]{:S(2)}, u32[]{:S(2)}) async-start(bf16[8,2,144,2048]{3,2,1,0:T(8,128)(2,1)} %bitcast.234), calls=%async_computation | async-start | bytes 18874368 | tf_op jit(solution)/shard_map/all_to_all | solution.py:145
  266.1 12.4 copy-start.23
  266.1 12.4 copy-start.62
  471.5 210.5 %all-to-all-start.2 = ((bf16[8,2,144,2048]{3,2,1,0:T(8,128)(2,1)}), bf16[8,2,144,2048]{3,2,1,0:T(8,128)(2,1)}, u32[]{:S(2)}, u32[]{:S(2)}) async-start(bf16[8,2,144,2048]{3,2,1,0:T(8,128)(2,1)} %multiply_convert_fusion), calls=%async_computation.2 | async-start | bytes 18874368 | tf_op jit(solution)/shard_map/all_to_all | solution.py:179
  476.6 994.7 %reduce-scatter.8.cloned.1.call-start = ((), (), s32[]{:S(2)}) async-start(), calls=%async_computation.10 | async-start | bytes 20971520 | tf_op jit(solution)/shard_map/reduce_scatter | solution.py:213
  723.0 748.3 %reduce-scatter.6.cloned.1.call-start = ((), (), s32[]{:S(2)}) async-start(), calls=%async_computation.9 | async-start | bytes 41943040 | tf_op jit(solution)/shard_map/reduce_scatter | solution.py:212
  780.1 209.8 %all-to-all-start.1 = ((bf16[8,2,144,2048]{3,2,1,0:T(8,128)(2,1)}), bf16[8,2,144,2048]{3,2,1,0:T(8,128)(2,1)}, u32[]{:S(2)}, u32[]{:S(2)}) async-start(bf16[8,2,144,2048]{3,2,1,0:T(8,128)(2,1)} %copy.197), calls=%async_computation.1 | async-start | bytes 18874368 | tf_op jit(solution)/shard_map/all_to_all | solution.py:155
  820.6 174.5 %copy-start.68 = (pred[2048]{0:T(1024)(128)(4,1)S(1)}, pred[2048]{0:T(1024)(128)(4,1)}, u32[]{:S(2)}) copy-start(pred[2048]{0:T(1024)(128)(4,1)} %get-tuple-element.13) | copy-start | bytes 6148
  820.6 174.7 %copy-start.54 = (f32[1,256,8]{1,2,0:T(8,128)S(1)}, f32[1,256,8]{1,2,0:T(8,128)}, u32[]{:S(2)}) copy-start(f32[1,256,8]{1,2,0:T(8,128)} %param.14) | copy-start | bytes 24580
  820.6 175.5 %copy-start.56 = (s32[2048,1]{0,1:T(1,128)S(1)}, s32[2048,1]{0,1:T(1,128)}, u32[]{:S(2)}) copy-start(s32[2048,1]{0,1:T(1,128)} %copy-done.55) | copy-start | bytes 24580
  820.6 175.5 %copy-start.64 = (f32[128]{0:T(128)S(1)}, f32[128]{0:T(128)}, u32[]{:S(2)}) copy-start(f32[128]{0:T(128)} %get-tuple-element.44) | copy-start | bytes 1540
  820.6 175.5 %copy-start.66 = (f32[128]{0:T(128)S(1)}, f32[128]{0:T(128)}, u32[]{:S(2)}) copy-start(f32[128]{0:T(128)} %get-tuple-element.43) | copy-start | bytes 1540
  820.6 176.1 %copy-start.37 = (f32[256,16]{0,1:T(8,128)S(1)}, f32[256,16]{0,1:T(8,128)}, u32[]{:S(2)}) copy-start(f32[256,16]{0,1:T(8,128)} %copy-done.36) | copy-start | bytes 49156
  820.6 176.2 %copy-start.39 = (f32[256,16]{0,1:T(8,128)S(1)}, f32[256,16]{0,1:T(8,128)}, u32[]{:S(2)}) copy-start(f32[256,16]{0,1:T(8,128)} %copy-done.38) | copy-start | bytes 49156
  820.6 176.3 %copy-start.47 = (f32[256,16]{0,1:T(8,128)S(1)}, f32[256,16]{0,1:T(8,128)}, u32[]{:S(2)}) copy-start(f32[256,16]{0,1:T(8,128)} %get-tuple-element.45) | copy-start | bytes 49156
  820.6 177.0 %copy-start.48 = (f32[256,16]{0,1:T(8,128)S(1)}, f32[256,16]{0,1:T(8,128)}, u32[]{:S(2)}) copy-start(f32[256,16]{0,1:T(8,128)} %get-tuple-element.47) | copy-start | bytes 49156
  989.9 209.5 %all-to-all-start.3 = ((bf16[8,2,144,2048]{3,2,1,0:T(8,128)(2,1)}), bf16[8,2,144,2048]{3,2,1,0:T(8,128)(2,1)}, u32[]{:S(2)}, u32[]{:S(2)}) async-start(bf16[8,2,144,2048]{3,2,1,0:T(8,128)(2,1)} %copy.202), calls=%async_computation.3 | async-start | bytes 18874368 | tf_op jit(solution)/shard_map/all_to_all | solution.py:198
  995.0 1813.4 %reduce-scatter.4.cloned.1.call-start = ((), (), s32[]{:S(2)}) async-start(), calls=%async_computation.8 | async-start | bytes 69206016 | tf_op jit(solution)/shard_map/reduce_scatter | solution.py:268
  1251.6 11.4 copy-start.8
  1251.6 11.4 copy-start.41
  1251.6 11.4 copy-start.60
  1266.3 12.7 copy-start.24
  1266.3 12.7 copy-start.63
  1310.5 5.7 copy-start.22
  1310.5 19.8 slice-start
  1316.1 14.2 slice-start.1
  1331.3 9.0 copy-start.10
  1331.3 9.0 copy-start.30
  1331.3 9.0 copy-start.46
  1405.1 14.8 copy-start.50
  1405.1 62.6 %copy-start.4 = (f32[256,2048]{1,0:T(8,128)S(1)}, f32[256,2048]{1,0:T(8,128)}, u32[]{:S(2)}) copy-start(f32[256,2048]{1,0:T(8,128)} %copy-done.3) | copy-start | bytes 6291460
  1405.1 62.6 %copy-start.69 = (f32[256]{0:T(256)S(1)}, f32[256]{0:T(256)}, u32[]{:S(2)}) copy-start(f32[256]{0:T(256)} %get-tuple-element.51) | copy-start | bytes 3076
  (32 other events, 58.9 us)
Sparse Core Ops, SparseCore 0:
  11.0 197.5 all-gather.1
  723.1 125.1 reduce-scatter.7
  851.6 234.8 reduce-scatter.5
  1405.2 1403.1 reduce-scatter.3
where the time goes:
time: 2820 us
  waiting for transfers between devices  2180 us (77%)
  matrix products  226 us (8%)
  local copies, waits for them, and re-layouts  194 us (7%)
  other arithmetic  128 us (5%)
  blocking collectives  47.2 us (2%)
    reduce_scatter x1, waiting for transfers between devices, on_device(): lax.psum_scatter(full_terms, ('dp', 'ep'), scatter_dimension=0, tiled=True)  1340 us
    all_to_all x1, waiting for transfers between devices, on_device(): lax.all_to_all(grad_rows.astype(jnp.bfloat16), 'ep', split_axis=0, concat...  192 us
    all_to_all x1, waiting for transfers between devices, on_device(): lax.all_to_all(slot_grad, 'ep', split_axis=0, concat_axis=0, tiled=True)  178 us
    all_to_all x1, waiting for transfers between devices, on_device(): lax.all_to_all(send_rows, 'ep', split_axis=0, concat_axis=0, tiled=True)  171 us
    all_to_all x1, waiting for transfers between devices, on_device(): lax.all_to_all(result.astype(jnp.bfloat16), 'ep', split_axis=0, concat_ax...  169 us
    all_gather x1, waiting for transfers between devices, on_device(): whole_weight = lax.all_gather(attn_weight, ('dp', 'ep'), axis=0, tiled=True)  135 us
  transfers between devices with their start and end apart: 8, of which 6 were waited for; matrix products, arithmetic and copies ran while one was open for 16% of the time, Pallas kernels for 0%

commit v1 on v0

--- a/solution.py
+++ b/solution.py
@@ -85,7 +85,24 @@
     gain_ffn = gains[model_width : 2 * model_width]
     gain_query = gains[2 * model_width : 2 * model_width + head_size]
     gain_key = gains[2 * model_width + head_size :]
-    whole_weight = lax.all_gather(attn_weight, ("dp", "ep"), axis=0, tiled=True)
+    part_next = lax.psum(1, ("dp", "ep"))
+    val = lax.axis_index(("dp", "ep"))
+    value_now, d_next, left_arr = (part_next, val, attn_weight.shape[0])
+    b_next, block_out = (attn_weight, 1)
+    while block_out < value_now:
+        b_next = jnp.concatenate(
+            [
+                b_next,
+                lax.ppermute(
+                    b_next,
+                    ("dp", "ep"),
+                    tuple(((dev_j, (dev_j - block_out) % value_now) for dev_j in range(value_now))),
+                ),
+            ],
+            axis=0,
+        )
+        block_out = 2 * block_out
+    whole_weight = jnp.roll(b_next, d_next * left_arr, axis=0)
     weight_qkv = whole_weight[:, : 3 * model_width]
     weight_out = whole_weight[:, 3 * model_width :]
     scale_first = inv_rms(inputs)

time: 2820 us -> 3390 us (1.20)
  waiting for transfers between devices: 2180 us -> 2680 us
  local copies, waits for them, and re-layouts: 194 us -> 253 us
    ppermute x0 -> x5, waiting for transfers between devices: none -> 631 us  [on_device(): lax.ppermute(b_next, ('dp', 'ep'), tuple(((dev_j, (dev_j - block_out) % v...]
    all_gather x1 -> x0, waiting for transfers between devices: 135 us -> none  [on_device(): whole_weight = lax.all_gather(attn_weight, ('dp', 'ep'), axis=0, tiled=True)]
    unnamed x152 -> x178, local copies, waits for them, and re-layouts: 13.2 us -> 49.1 us
  transfers between devices with their start and end apart: 8 -> 12, of which waited for: 6 -> 10; matrix products, arithmetic and copies ran while one was open for 16% -> 14% of each run, Pallas kernels for 0% -> 0%
where the time goes in v1:
time: 3390 us
  waiting for transfers between devices  2680 us (79%)
  local copies, waits for them, and re-layouts  253 us (7%)
  matrix products  229 us (7%)
  other arithmetic  135 us (4%)
  blocking collectives  50 us (1%)
    reduce_scatter x1, waiting for transfers between devices, on_device(): lax.psum_scatter(full_terms, ('dp', 'ep'), scatter_dimension=0, tiled=True)  1330 us
    ppermute x5, waiting for transfers between devices, on_device(): lax.ppermute(b_next, ('dp', 'ep'), tuple(((dev_j, (dev_j - block_out) % v...  631 us
    all_to_all x1, waiting for transfers between devices, on_device(): lax.all_to_all(grad_rows.astype(jnp.bfloat16), 'ep', split_axis=0, concat...  192 us
    all_to_all x1, waiting for transfers between devices, on_device(): lax.all_to_all(slot_grad, 'ep', split_axis=0, concat_axis=0, tiled=True)  178 us
    all_to_all x1, waiting for transfers between devices, on_device(): lax.all_to_all(send_rows, 'ep', split_axis=0, concat_axis=0, tiled=True)  171 us
    all_to_all x1, waiting for transfers between devices, on_device(): lax.all_to_all(result.astype(jnp.bfloat16), 'ep', split_axis=0, concat_ax...  169 us
  transfers between devices with their start and end apart: 12, of which 10 were waited for; matrix products, arithmetic and copies ran while one was open for 14% of the time, Pallas kernels for 0%

profile of v1, /device:TPU:0, one launch (start us, length us, event | category | flops | bytes accessed | tf_op | source)
XLA Modules:
  0.0 3387.7 jit_solution(8972432696100122534)
XLA Ops:
  7.2 6.4 collective-permute-start
  13.6 22.9 collective-permute-done
  38.8 46.3 %collective-permute-done.1 = bf16[128,8192]{1,0:T(8,128)(2,1)S(1)} collective-permute-done((bf16[128,8192]{1,0:T(8,128)(2,1)S(1)}, bf16[128,8192]{1,0:T(8,128)(2,1)S(1)}, u32[]{:S(2)}, u32[]{:S(2)}) %collective-permute-start.1) | collective-permute-done | bytes 2097184 | tf_op jit(solution)/shard_map/ppermute | solution.py:96
  85.5 182.9 %collective-permute-done.2 = bf16[256,8192]{1,0:T(8,128)(2,1)S(1)} collective-permute-done((bf16[256,8192]{1,0:T(8,128)(2,1)S(1)}, bf16[256,8192]{1,0:T(8,128)(2,1)S(1)}, u32[]{:S(2)}, u32[]{:S(2)}) %collective-permute-start.2) | collective-permute-done | bytes 4194336 | tf_op jit(solution)/shard_map/ppermute | solution.py:96
  283.5 81.5 %collective-permute-done.3 = bf16[512,8192]{1,0:T(8,128)(2,1)S(1)} collective-permute-done((bf16[512,8192]{1,0:T(8,128)(2,1)}, bf16[512,8192]{1,0:T(8,128)(2,1)S(1)}, u32[]{:S(2)}, u32[]{:S(2)}) %collective-permute-start.3) | collective-permute-done | bytes 8388640 | tf_op jit(solution)/shard_map/ppermute | solution.py:96
  365.0 7.3 constant_dynamic-update-slice_fusion
  375.5 8.0 scatter_custom_fusion
  383.6 13.1 gather_fusion.1
  396.7 11.8 gather_fusion
  414.2 11.8 gather_fusion.2
  426.0 8.6 scatter_custom_fusion.1
  439.6 297.0 %collective-permute-done.4 = bf16[1024,8192]{1,0:T(8,128)(2,1)} collective-permute-done((bf16[1024,8192]{1,0:T(8,128)(2,1)}, bf16[1024,8192]{1,0:T(8,128)(2,1)}, u32[]{:S(2)}, u32[]{:S(2)}) %collective-permute-start.4) | collective-permute-done | bytes 16777248 | tf_op jit(solution)/shard_map/ppermute | solution.py:96
  736.6 14.0 constant_dynamic-update-slice_fusion.11
  756.6 7.6 constant_dynamic-update-slice_fusion.6
  764.2 14.0 constant_dynamic-update-slice_fusion.5
  778.2 11.7 fusion.2
  811.9 6.2 multiply_reduce_fusion.3
  819.8 9.9 gather_fusion.3
  829.7 6.1 all-to-all-start
  836.7 12.3 gather_fusion.6
  849.6 11.5 gather_fusion.5
  861.1 9.9 multiply_convert_fusion
  871.0 171.4 %all-to-all-done = bf16[8,2,144,2048]{3,2,1,0:T(8,128)(2,1)} async-done(((bf16[8,2,144,2048]{3,2,1,0:T(8,128)(2,1)}), bf16[8,2,144,2048]{3,2,1,0:T(8,128)(2,1)}, u32[]{:S(2)}, u32[]{:S(2)}) %all-to-all-start) | async-done | bytes 9437216 | tf_op jit(solution)/shard_map/all_to_all | solution.py:162
  1047.6 27.5 fusion.27
  1075.1 178.1 %all-to-all-done.2 = bf16[8,2,144,2048]{3,2,1,0:T(8,128)(2,1)} async-done(((bf16[8,2,144,2048]{3,2,1,0:T(8,128)(2,1)}), bf16[8,2,144,2048]{3,2,1,0:T(8,128)(2,1)}, u32[]{:S(2)}, u32[]{:S(2)}) %all-to-all-start.2) | async-done | bytes 9437216 | tf_op jit(solution)/shard_map/all_to_all | solution.py:196
  1253.2 22.8 fusion.11
  1276.0 18.5 fusion.32
  1294.6 31.7 convolution_bitcast_fusion
  1326.3 16.4 convert_bitcast_fusion.1
  1342.7 9.3 copy.197
  1357.3 25.7 convert_bitcast_fusion
  1383.0 9.5 copy.202
  1392.5 169.3 %all-to-all-done.1 = bf16[8,2,144,2048]{3,2,1,0:T(8,128)(2,1)} async-done(((bf16[8,2,144,2048]{3,2,1,0:T(8,128)(2,1)}), bf16[8,2,144,2048]{3,2,1,0:T(8,128)(2,1)}, u32[]{:S(2)}, u32[]{:S(2)}) %all-to-all-start.1) | async-done | bytes 9437216 | tf_op jit(solution)/shard_map/all_to_all | solution.py:172
  1569.7 9.4 concatenate.76
  1579.1 192.2 %all-to-all-done.3 = bf16[8,2,144,2048]{3,2,1,0:T(8,128)(2,1)} async-done(((bf16[8,2,144,2048]{3,2,1,0:T(8,128)(2,1)}), bf16[8,2,144,2048]{3,2,1,0:T(8,128)(2,1)}, u32[]{:S(2)}, u32[]{:S(2)}) %all-to-all-start.3) | async-done | bytes 9437216 | tf_op jit(solution)/shard_map/all_to_all | solution.py:215
  1771.3 9.3 concatenate.80
  1780.6 21.2 gather_fusion.4
  1801.8 21.5 gather_fusion.7
  1823.3 11.5 convert_reduce_fusion
  1838.0 13.0 fusion.4
  1856.4 5.8 fusion.42
  1890.7 10.2 fusion.76
  1904.6 9.0 fusion.61
  1913.6 21.6 fusion.66
  1935.2 43.3 %pad_maximum_fusion = f32[2048,8192]{1,0:T(8,128)} fusion(f32[2048,2048]{1,0:T(8,128)} %fusion.76, f32[2048,6144]{1,0:T(8,128)} %fusion.66), kind=kLoop, calls=%fused_computation.10 | loop fusion | flops 16777216 | bytes 134217728 | tf_op jit(solution)/shard_map/concatenate | solution.py:283
  1978.6 14.7 fusion.55
  1993.3 50.0 %all-reduce.4 = f32[4352]{0:T(1024)S(1)} all-reduce(f32[4352]{0:T(1024)S(1)} %pad_maximum_fusion.16), channel_id=3, replica_groups=mesh['dp'=4,'ep'=8] {'dp','ep'}, use_global_device_ids=true, to_apply=%region_25.26.clone | all-reduce | flops 4352 | bytes 34816
  2047.5 1333.5 %reduce-scatter.4.cloned.1.call-done = f32[64,8192]{1,0:T(8,128)} async-done(((f32[2048,8192]{1,0:T(8,128)}), f32[64,8192]{1,0:T(8,128)}) %reduce-scatter.4.cloned.1.call-update) | async-done | bytes 2097168 | tf_op jit(solution)/shard_map/reduce_scatter | solution.py:285
  (278 shorter events, 124.8 us)
Async XLA Ops:
  7.2 77.9 %copy-start.5 = (bf16[64,8192]{1,0:T(8,128)(2,1)S(1)}, bf16[64,8192]{1,0:T(8,128)(2,1)}, u32[]{:S(2)}) copy-start(bf16[64,8192]{1,0:T(8,128)(2,1)} %param.15) | copy-start | bytes 3145732
  7.2 29.3 collective-permute-start
  36.5 238.7 %copy-start.6 = (bf16[64,8192]{1,0:T(8,128)(2,1)}, bf16[64,8192]{1,0:T(8,128)(2,1)S(1)}, u32[]{:S(2)}) copy-start(bf16[64,8192]{1,0:T(8,128)(2,1)S(1)} %collective-permute-done) | copy-start | bytes 3145732
  38.3 46.7 %collective-permute-start.1 = (bf16[128,8192]{1,0:T(8,128)(2,1)S(1)}, bf16[128,8192]{1,0:T(8,128)(2,1)S(1)}, u32[]{:S(2)}, u32[]{:S(2)}) collective-permute-start(bf16[128,8192]{1,0:T(8,128)(2,1)S(1)} %pad_maximum_fusion.5), channel_id=1, source_target_pairs={{0,30},{1,31},{2,0},{3,1},{4,2},{5,3},{6,4},{7,5},{8,6},{9,7},{10,... | collective-permute-start | bytes 6291464 | tf_op jit(solution)/shard_map/ppermute | solution.py:96
  85.4 183.0 %collective-permute-start.2 = (bf16[256,8192]{1,0:T(8,128)(2,1)S(1)}, bf16[256,8192]{1,0:T(8,128)(2,1)S(1)}, u32[]{:S(2)}, u32[]{:S(2)}) collective-permute-start(bf16[256,8192]{1,0:T(8,128)(2,1)S(1)} %pad_maximum_fusion.3), channel_id=1, source_target_pairs={{0,28},{1,29},{2,30},{3,31},{4,0},{5,1},{6,2},{7,3},{8,4},{9,5},{1... | collective-permute-start | bytes 12582920 | tf_op jit(solution)/shard_map/ppermute | solution.py:96
  268.4 10.8 copy-start.2
  272.7 92.3 %collective-permute-start.3 = (bf16[512,8192]{1,0:T(8,128)(2,1)}, bf16[512,8192]{1,0:T(8,128)(2,1)S(1)}, u32[]{:S(2)}, u32[]{:S(2)}) collective-permute-start(bf16[512,8192]{1,0:T(8,128)(2,1)} %pad_maximum_fusion.2), channel_id=1, source_target_pairs={{0,24},{1,25},{2,26},{3,27},{4,28},{5,29},{6,30},{7,31},{8,0},{9,1... | collective-permute-start | bytes 25165832 | tf_op jit(solution)/shard_map/ppermute | solution.py:96
  365.0 10.5 copy-start.75
  373.4 363.1 %collective-permute-start.4 = (bf16[1024,8192]{1,0:T(8,128)(2,1)}, bf16[1024,8192]{1,0:T(8,128)(2,1)}, u32[]{:S(2)}, u32[]{:S(2)}) collective-permute-start(bf16[1024,8192]{1,0:T(8,128)(2,1)} %get-tuple-element.19), channel_id=1, source_target_pairs={{0,16},{1,17},{2,18},{3,19},{4,20},{5,21},{6,22},{7,23},{8,24},{9,... | collective-permute-start | bytes 50331656 | tf_op jit(solution)/shard_map/ppermute | solution.py:96
  414.2 23.8 copy-start.67
  426.0 12.5 copy-start.48
  426.0 12.4 copy-start.61
  435.2 373.5 %copy-start.63 = (pred[256]{0:T(512)(128)(4,1)}, pred[256]{0:T(512)(128)(4,1)S(1)}, u32[]{:S(2)}) copy-start(pred[256]{0:T(512)(128)(4,1)S(1)} %get-tuple-element.74) | copy-start | bytes 772
  437.9 340.2 %copy-start.50 = (f32[256]{0:T(256)}, f32[256]{0:T(256)S(1)}, u32[]{:S(2)}) copy-start(f32[256]{0:T(256)S(1)} %get-tuple-element.62) | copy-start | bytes 3076
  439.1 339.1 %copy-start.35 = (f32[2048]{0:T(1024)}, f32[2048]{0:T(1024)S(1)}, u32[]{:S(2)}) copy-start(f32[2048]{0:T(1024)S(1)} %get-tuple-element.52) | copy-start | bytes 24580
  439.6 364.7 %copy-start.31 = (f32[256,64]{1,0:T(8,128)}, f32[256,64]{1,0:T(8,128)S(1)}, u32[]{:S(2)}) copy-start(f32[256,64]{1,0:T(8,128)S(1)} %get-tuple-element.65) | copy-start | bytes 196612
  439.6 364.7 %copy-start.33 = (f32[256,64]{1,0:T(8,128)}, f32[256,64]{1,0:T(8,128)S(1)}, u32[]{:S(2)}) copy-start(f32[256,64]{1,0:T(8,128)S(1)} %get-tuple-element.66) | copy-start | bytes 196612
  736.6 15.1 copy-start.7
  764.2 14.0 copy-start.16
  829.7 212.7 %all-to-all-start = ((bf16[8,2,144,2048]{3,2,1,0:T(8,128)(2,1)}), bf16[8,2,144,2048]{3,2,1,0:T(8,128)(2,1)}, u32[]{:S(2)}, u32[]{:S(2)}) async-start(bf16[8,2,144,2048]{3,2,1,0:T(8,128)(2,1)} %bitcast.232), calls=%async_computation | async-start | bytes 18874368 | tf_op jit(solution)/shard_map/all_to_all | solution.py:162
  836.7 12.4 copy-start.29
  836.7 12.4 copy-start.68
  1042.4 210.8 %all-to-all-start.2 = ((bf16[8,2,144,2048]{3,2,1,0:T(8,128)(2,1)}), bf16[8,2,144,2048]{3,2,1,0:T(8,128)(2,1)}, u32[]{:S(2)}, u32[]{:S(2)}) async-start(bf16[8,2,144,2048]{3,2,1,0:T(8,128)(2,1)} %multiply_convert_fusion), calls=%async_computation.2 | async-start | bytes 18874368 | tf_op jit(solution)/shard_map/all_to_all | solution.py:196
  1047.5 999.9 %reduce-scatter.8.cloned.1.call-start = ((), (), s32[]{:S(2)}) async-start(), calls=%async_computation.9 | async-start | bytes 20971520 | tf_op jit(solution)/shard_map/reduce_scatter | solution.py:230
  1294.5 753.0 %reduce-scatter.6.cloned.1.call-start = ((), (), s32[]{:S(2)}) async-start(), calls=%async_computation.8 | async-start | bytes 41943040 | tf_op jit(solution)/shard_map/reduce_scatter | solution.py:229
  1352.1 209.8 %all-to-all-start.1 = ((bf16[8,2,144,2048]{3,2,1,0:T(8,128)(2,1)}), bf16[8,2,144,2048]{3,2,1,0:T(8,128)(2,1)}, u32[]{:S(2)}, u32[]{:S(2)}) async-start(bf16[8,2,144,2048]{3,2,1,0:T(8,128)(2,1)} %copy.197), calls=%async_computation.1 | async-start | bytes 18874368 | tf_op jit(solution)/shard_map/all_to_all | solution.py:172
  1392.5 174.5 %copy-start.76 = (pred[2048]{0:T(1024)(128)(4,1)S(1)}, pred[2048]{0:T(1024)(128)(4,1)}, u32[]{:S(2)}) copy-start(pred[2048]{0:T(1024)(128)(4,1)} %get-tuple-element.13) | copy-start | bytes 6148
  1392.5 174.7 %copy-start.59 = (f32[1,256,8]{1,2,0:T(8,128)S(1)}, f32[1,256,8]{1,2,0:T(8,128)}, u32[]{:S(2)}) copy-start(f32[1,256,8]{1,2,0:T(8,128)} %param.14) | copy-start | bytes 24580
  1392.5 175.6 %copy-start.62 = (s32[2048,1]{0,1:T(1,128)S(1)}, s32[2048,1]{0,1:T(1,128)}, u32[]{:S(2)}) copy-start(s32[2048,1]{0,1:T(1,128)} %copy-done.61) | copy-start | bytes 24580
  1392.5 175.6 %copy-start.71 = (f32[128]{0:T(128)S(1)}, f32[128]{0:T(128)}, u32[]{:S(2)}) copy-start(f32[128]{0:T(128)} %get-tuple-element.53) | copy-start | bytes 1540
  1392.5 175.6 %copy-start.73 = (f32[128]{0:T(128)S(1)}, f32[128]{0:T(128)}, u32[]{:S(2)}) copy-start(f32[128]{0:T(128)} %get-tuple-element.54) | copy-start | bytes 1540
  1392.5 176.2 %copy-start.42 = (f32[256,16]{0,1:T(8,128)S(1)}, f32[256,16]{0,1:T(8,128)}, u32[]{:S(2)}) copy-start(f32[256,16]{0,1:T(8,128)} %get-tuple-element.56) | copy-start | bytes 49156
  1392.5 176.2 %copy-start.44 = (f32[256,16]{0,1:T(8,128)S(1)}, f32[256,16]{0,1:T(8,128)}, u32[]{:S(2)}) copy-start(f32[256,16]{0,1:T(8,128)} %copy-done.43) | copy-start | bytes 49156
  1392.5 176.3 %copy-start.52 = (f32[256,16]{0,1:T(8,128)S(1)}, f32[256,16]{0,1:T(8,128)}, u32[]{:S(2)}) copy-start(f32[256,16]{0,1:T(8,128)} %get-tuple-element.55) | copy-start | bytes 49156
  1392.5 177.1 %copy-start.53 = (f32[256,16]{0,1:T(8,128)S(1)}, f32[256,16]{0,1:T(8,128)}, u32[]{:S(2)}) copy-start(f32[256,16]{0,1:T(8,128)} %get-tuple-element.57) | copy-start | bytes 49156
  1561.8 209.4 %all-to-all-start.3 = ((bf16[8,2,144,2048]{3,2,1,0:T(8,128)(2,1)}), bf16[8,2,144,2048]{3,2,1,0:T(8,128)(2,1)}, u32[]{:S(2)}, u32[]{:S(2)}) async-start(bf16[8,2,144,2048]{3,2,1,0:T(8,128)(2,1)} %copy.202), calls=%async_computation.3 | async-start | bytes 18874368 | tf_op jit(solution)/shard_map/all_to_all | solution.py:215
  1566.9 1814.0 %reduce-scatter.4.cloned.1.call-start = ((), (), s32[]{:S(2)}) async-start(), calls=%async_computation.7 | async-start | bytes 69206016 | tf_op jit(solution)/shard_map/reduce_scatter | solution.py:285
  1823.3 11.5 copy-start.15
  1823.3 11.5 copy-start.46
  1823.3 11.5 copy-start.66
  1838.0 13.0 copy-start.30
  1838.0 13.0 copy-start.69
  1883.7 20.9 slice-start
  1890.7 10.8 copy-start.39
  1890.7 13.9 slice-start.1
  1978.6 14.8 copy-start.55
  1978.6 65.4 %copy-start.10 = (f32[256,2048]{1,0:T(8,128)S(1)}, f32[256,2048]{1,0:T(8,128)}, u32[]{:S(2)}) copy-start(f32[256,2048]{1,0:T(8,128)} %copy-done.9) | copy-start | bytes 6291460
  1978.6 65.4 %copy-start.77 = (f32[256]{0:T(256)S(1)}, f32[256]{0:T(256)}, u32[]{:S(2)}) copy-start(f32[256]{0:T(256)} %get-tuple-element.61) | copy-start | bytes 3076
  (44 other events, 189.0 us)
Sparse Core Ops, SparseCore 0:
  1294.6 124.2 reduce-scatter.7
  1422.2 234.8 reduce-scatter.5
  1978.6 1402.2 reduce-scatter.3
